TPU v7x, 32 devices: a whole 2x2x4 slice. The times are simulated.
32 devices in a mesh: books: 2 (over x), wide: 4 (over y, core), narrow: 4 (over z).
Axes of the slice: x: 2, y: 2, z: 4, core: 2. Of those that a mesh axis runs over, the one named last changes fastest.
Arguments:
- dec_queries: bfloat16 [16384, 1024], P(('books', 'wide', 'narrow')), parts along dimension 0, may hold values from -6 to 6
- dec_keys: bfloat16 [16384, 1024], P(('books', 'wide', 'narrow')), parts along dimension 0, may hold values from -6 to 6
- dec_values: bfloat16 [16384, 1024], P(('books', 'wide', 'narrow')), parts along dimension 0, may hold values from -6 to 6
- enc_keys: bfloat16 [16384, 1024], P(('books', 'wide', 'narrow')), parts along dimension 0, may hold values from -6 to 6
- enc_values: bfloat16 [16384, 1024], P(('books', 'wide', 'narrow')), parts along dimension 0, may hold values from -6 to 6
- out_weight: bfloat16 [1024, 2048], replicated, may hold values from -0.1875 to 0.1875
- head_gain: float32 [1024], replicated, may hold values from 0.1 to 1.9
Outputs:
- output: bfloat16 [16384, 2048], P(('books', 'wide', 'narrow')), parts along dimension 0
There are 2 independent parts, one for each index of `books`. A program takes and returns all parts, laid end to end along the dimension named above; an argument that names none is the same for every part. Nothing has to cross between parts.
All inputs are finite; a program needn't handle non-finite values.
Results may differ from a plain program's by a relative error of at most 0.0058.
Values sent between devices are 32-bit elements; how exact they have to be, the bound alone decides.
A program may use at most 128 MiB of HBM per device.

v0:
```python
import jax
import jax.numpy as jnp
from jax import lax
from jax.sharding import PartitionSpec as P

HEADS = 8
HEAD_DIM = 128
BLOCK = 128


def carried_in(part, axis, combine, identity):
    place = lax.axis_index(axis)
    gathered = lax.all_gather(part, axis)
    state = jnp.zeros_like(part) + jnp.asarray(identity, part.dtype)

    def one(lap, state):
        return combine(state, lax.dynamic_index_in_dim(gathered, lap, 0, False))

    return lax.fori_loop(0, place, one, state)


def combine_sum(earlier, later):
    return earlier + later


def local(dec_queries, dec_keys, dec_values, enc_keys, enc_values, out_weight, head_gain):
    tokens = dec_queries.shape[0]
    block_count = tokens // BLOCK
    queries = dec_queries.reshape(block_count, BLOCK, HEADS, HEAD_DIM)
    keys_dec = dec_keys.reshape(block_count, BLOCK, HEADS, HEAD_DIM)
    values_dec = dec_values.reshape(block_count, BLOCK, HEADS, HEAD_DIM)
    enc_part = jnp.einsum(
        "thd,the->hde",
        enc_keys.reshape(tokens, HEADS, HEAD_DIM),
        enc_values.reshape(tokens, HEADS, HEAD_DIM),
        preferred_element_type=jnp.float32,
    )
    block_states = jnp.einsum(
        "nchd,nche->nhde", keys_dec, values_dec, preferred_element_type=jnp.float32
    )
    own_total = jnp.sum(block_states, axis=0)
    earlier_local = jnp.cumsum(block_states, axis=0) - block_states
    identity = jnp.zeros_like(own_total)
    inner = carried_in(own_total, "narrow", combine_sum, identity)
    group_dec, group_enc = lax.psum((own_total, enc_part), "narrow")
    outer = carried_in(group_dec, "wide", combine_sum, identity)
    memory = lax.psum(group_enc, "wide")
    before = inner + outer
    rows = lax.broadcasted_iota(jnp.int32, (BLOCK, BLOCK), 0)
    columns = lax.broadcasted_iota(jnp.int32, (BLOCK, BLOCK), 1)
    causal = rows >= columns
    scores = jnp.einsum("nchd,nshd->nhcs", queries, keys_dec, preferred_element_type=jnp.float32)
    scores_bf = jnp.where(causal[None, None], scores, 0.0).astype(jnp.bfloat16)
    within_block = jnp.einsum(
        "nhcs,nshe->nche", scores_bf, values_dec, preferred_element_type=jnp.float32
    )
    carried = ((memory + before)[None] + earlier_local).astype(jnp.bfloat16)
    from_state = jnp.einsum("nchd,nhde->nche", queries, carried, preferred_element_type=jnp.float32)
    attended = within_block + from_state
    inverse = lax.rsqrt(jnp.mean(attended * attended, axis=-1, keepdims=True) + 1e-06)
    gain = head_gain.reshape(HEADS, HEAD_DIM)
    normed = (attended * inverse * gain).astype(jnp.bfloat16).reshape(tokens, HEADS * HEAD_DIM)
    return jnp.dot(normed, out_weight, preferred_element_type=jnp.float32).astype(jnp.bfloat16)


def solution(mesh):
    placed = (
        P(("books", "wide", "narrow"), None),
        P(("books", "wide", "narrow"), None),
        P(("books", "wide", "narrow"), None),
        P(("books", "wide", "narrow"), None),
        P(("books", "wide", "narrow"), None),
        P(),
        P(),
    )
    return jax.shard_map(
        local,
        mesh=mesh,
        in_specs=placed,
        out_specs=P(("books", "wide", "narrow"), None),
        check_vma=False,
    )
```

profile of v0, /device:TPU:0, one launch (start us, length us, event | category | flops | bytes accessed | tf_op | source)
XLA Modules:
  0.0 192.9 jit_solution(5654450518963406215)
XLA Ops:
  6.5 1.6 copy.33
  8.1 0.8 copy.24
  8.9 1.5 copy.34
  10.4 2.6 %fusion.15 = (f32[8,128,128]{2,1,0:T(8,128)}, f32[4,8,128,128]{3,2,1,0:T(8,128)}) fusion(bf16[4,128,8,128]{1,3,2,0:T(8,128)(2,1)S(1)} %copy.24, bf16[4,128,8,128]{3,2,1,0:T(8,128)(2,1)S(1)} %bitcast.45), kind=kOutput, calls=%fused_computation.25 | convolution fusion | flops 134610944 | bytes 4718592 | tf_op jit(solution)/shard_map/nchd,nche->nhde/dot_general | solution.py:38
  13.0 0.0 all-gather.6.cloned.1.call-update
  13.1 1.5 copy.30
  14.6 1.3 fusion.3
  15.8 46.0 %all-gather.6.cloned.1.call-done = f32[32,128,128]{2,1,0:T(8,128)} async-done(((f32[8,128,128]{2,1,0:T(8,128)}), f32[32,128,128]{2,1,0:T(8,128)}) %all-gather.6.cloned.1.call-update) | async-done | bytes 2097168 | tf_op jit(solution)/shard_map/all_gather | solution.py:13
  61.9 0.7 all-reduce.6.cloned.1.call-update
  62.6 0.0 all-gather.4.cloned.1.call-start
  62.6 53.4 %all-reduce.6.cloned.1.call-done = (f32[8,128,128]{2,1,0:T(8,128)}, f32[1,8,128,128]{3,2,1,0:T(8,128)}) async-done(((f32[8,128,128]{2,1,0:T(8,128)}, f32[1,8,128,128]{3,2,1,0:T(8,128)}), (f32[8,128,128]{2,1,0:T(8,128)}, f32[1,8,128,128]{3,2,1,0:T(8,128)})) %all-reduce.6.cloned.1.call-update) | async-done | bytes 1048592 | tf_op jit(solution)/shard_map/psum | solution.py:45
  116.1 0.0 all-reduce.4.cloned.1.call-start
  116.1 1.5 copy.32
  117.6 3.7 %fusion = f32[4,8,128,128]{2,3,1,0:T(8,128)} fusion(bf16[4,128,8,128]{1,3,2,0:T(8,128)(2,1)S(1)} %copy.24, pred[128,128]{1,0:T(8,128)(4,1)S(1)} %iota_compare_fusion, bf16[4,128,8,128]{3,2,1,0:T(8,128)(2,1)} %bitcast.46, bf16[4,128,8,128]{3,2,1,0:T(8,128)(2,1)S(1)} %bitcast.43), kind=kOutput, calls=%fused_computation.8 | convolution fusion | flops 269484032 | bytes 5259264 | tf_op jit(solution)/shard_map/nhcs,nshe->nche/dot_general | solution.py:54
  121.4 18.2 %all-gather.4.cloned.1.call-done = f32[4,8,128,128]{3,2,1,0:T(8,128)} async-done(((f32[1,8,128,128]{3,2,1,0:T(8,128)}), f32[4,8,128,128]{3,2,1,0:T(8,128)}) %all-gather.4.cloned.1.call-update) | async-done | bytes 2097168 | tf_op jit(solution)/shard_map/all_gather | solution.py:13
  139.7 35.5 %all-reduce.4.cloned.1.call-done = f32[8,128,128]{2,1,0:T(8,128)} async-done(((f32[8,128,128]{2,1,0:T(8,128)}), f32[8,128,128]{2,1,0:T(8,128)}) %all-reduce.4.cloned.1.call-update) | async-done | bytes 524304 | tf_op jit(solution)/shard_map/psum | solution.py:47
  175.2 1.3 add_add_fusion
  176.5 0.5 copy-done.1
  176.9 0.3 add_convert_fusion
  177.3 1.3 copy-done.3
  178.5 0.9 multiply_reduce_fusion
  179.5 0.4 multiply_convert_fusion
  179.8 0.7 copy.28
  180.6 5.8 %convolution_convert_fusion = bf16[512,2048]{1,0:T(8,128)(2,1)} fusion(bf16[1024,2048]{1,0:T(8,128)(2,1)} %param.16, bf16[64,8,8,128]{3,2,1,0:T(8,128)(2,1)S(1)} %bitcast.54), kind=kOutput, calls=%fused_computation.2 | convolution fusion | flops 2148532224 | bytes 7340032 | tf_op jit(solution)/shard_map/dot_general | solution.py:63
  (18 shorter events, 0.2 us)
Async XLA Ops:
  6.5 8.0 %copy-start = (bf16[512,1024]{1,0:T(8,128)(2,1)S(1)}, bf16[512,1024]{1,0:T(8,128)(2,1)}, u32[]{:S(2)}) copy-start(bf16[512,1024]{1,0:T(8,128)(2,1)} %param.15) | copy-start | bytes 3145732
  6.5 55.3 %all-gather.6.cloned.1.call-start = ((), (), s32[]{:S(2)}) async-start(), calls=%async_computation.2 | async-start | bytes 2621440 | tf_op jit(solution)/shard_map/all_gather | solution.py:13
  10.4 2.6 %copy-start.2 = (bf16[64,8,8,128]{3,2,1,0:T(8,128)(2,1)}, bf16[64,8,8,128]{3,2,1,0:T(8,128)(2,1)S(1)}, u32[]{:S(2)}) copy-start(bf16[64,8,8,128]{3,2,1,0:T(8,128)(2,1)S(1)} %copy.34) | copy-start | bytes 3145732
  61.8 54.2 %all-reduce.6.cloned.1.call-start = ((), (), s32[]{:S(2)}) async-start(), calls=%async_computation.3 | async-start | bytes 2097152 | tf_op jit(solution)/shard_map/psum | solution.py:45
  62.6 77.1 %all-gather.4.cloned.1.call-start = ((), (), s32[]{:S(2)}) async-start(), calls=%async_computation.1 | async-start | bytes 2621440 | tf_op jit(solution)/shard_map/all_gather | solution.py:13
  116.1 59.1 %all-reduce.4.cloned.1.call-start = ((), (), s32[]{:S(2)}) async-start(), calls=%async_computation | async-start | bytes 1048576 | tf_op jit(solution)/shard_map/psum | solution.py:47
  175.2 1.7 copy-start.1
  176.9 1.6 copy-start.3
  178.5 0.9 copy-start.4
Sparse Core Ops, SparseCore 0:
  13.2 48.6 all-gather.5
  65.1 50.8 all-reduce.5
  117.7 21.9 all-gather.3
  142.0 33.1 all-reduce.3
where the time goes:
time: 194 us; the launch traced here: 193 us
  waiting for transfers between devices  154 us (79%)
  matrix products  14.3 us (7%)
  between operations  13.3 us (7%)
  local copies, waits for them, and re-layouts  9.38 us (5%)
  other arithmetic  2.01 us (1%)
    all_gather x2, waiting for transfers between devices, carried_in(): gathered = lax.all_gather(part, axis)  64.3 us
    psum x1, waiting for transfers between devices, local(): group_dec, group_enc = lax.psum((own_total, enc_part), 'narrow')  53.4 us
    psum x1, waiting for transfers between devices, local(): memory = lax.psum(group_enc, 'wide')  35.5 us
    unnamed x13, local copies, waits for them, and re-layouts  6.3 us
    dot_general x1, matrix products, local(): jnp.dot(normed, out_weight, preferred_element_type=jnp.float32)  5.85 us
  transfers between devices with their start and end apart: 4, of which 4 were waited for; matrix products, arithmetic and copies ran while one was open for 4% of the time, Pallas kernels for 0%

commit v1 on v0

v1 whole, which is shorter than its diff:
```python
import functools

import jax
import jax.numpy as jnp
from jax import lax
from jax.experimental import pallas as pl
from jax.experimental.pallas import tpu as pltpu
from jax.sharding import PartitionSpec as P

HEADS = 8
HEAD_DIM = 128
BLOCK = 128
WIDE_LAG = 1
NARROW_LAG = 2
MESH = pl.DeviceIdType.MESH


def dot(a, b, contract):
    return lax.dot_general(a, b, (contract, ((), ())), preferred_element_type=jnp.float32)


def kernel(
    wide, narrow,
    q_hbm, dk_hbm, dv_hbm, ek_hbm, ev_hbm, gain_ref, out_ref,
    q, dk, dv, ek, ev, scores, enc, cum, base,
    f_out, g_out, p_out, r_out, f_in, g_in, p_in, r_in,
    load_sem, send_sem, recv_sem,
):
    w = lax.axis_index("wide")
    z = lax.axis_index("narrow")
    tokens = q.shape[1]
    blocks = tokens // BLOCK
    span = 2 * BLOCK if blocks % 2 == 0 else BLOCK

    def load(i, h):
        src, dst = ((ek_hbm, ek), (ev_hbm, ev), (dk_hbm, dk), (dv_hbm, dv), (q_hbm, q))[i]
        columns = pl.ds(pl.multiple_of(h * HEAD_DIM, HEAD_DIM), HEAD_DIM)
        return pltpu.make_async_copy(src.at[:, columns], dst.at[h], load_sem.at[i, h])

    barrier = pltpu.get_barrier_semaphore()
    has = (w > 0, w < wide - 1, z > 0, z < narrow - 1)
    peers = ({"wide": w - 1}, {"wide": w + 1}, {"narrow": z - 1}, {"narrow": z + 1})
    for there, peer in zip(has, peers):

        @pl.when(there)
        def _():
            pl.semaphore_signal(barrier, inc=1, device_id=peer, device_id_type=MESH)

    for h in range(HEADS):
        for i in range(4):
            load(i, h).start()
    for h in range(HEADS):
        load(4, h).start()

    for there, ref in zip(has, (f_in, g_in, p_in, r_in)):

        @pl.when(jnp.logical_not(there))
        def _():
            ref[...] = jnp.zeros_like(ref)

    pl.semaphore_wait(barrier, sum(there.astype(jnp.int32) for there in has))

    chains = (
        (f_out, f_in, 0, 1),
        (g_out, g_in, 1, 0),
        (p_out, p_in, 2, 3),
        (r_out, r_in, 3, 2),
    )

    def remote(c, h):
        out, into, _, to = chains[c]
        return pltpu.make_async_remote_copy(
            src_ref=out.at[h],
            dst_ref=into.at[h],
            send_sem=send_sem.at[c, h],
            recv_sem=recv_sem.at[c, h],
            device_id=peers[to],
            device_id_type=MESH,
        )

    def inside(h):
        return jnp.logical_and(h >= 0, h < HEADS)

    def link(c, h, value):
        out, into, source, to = chains[c]

        @pl.when(inside(h))
        def _():
            @pl.when(has[source])
            def _():
                remote(c, h).wait_recv()

            @pl.when(has[to])
            def _():
                out[h] = into[h] + value(h)
                remote(c, h).start()

    def states(h):
        for i in range(4):
            load(i, h).wait()
        enc[h] = dot(ek[h], ev[h], ((0,), (0,)))
        total = None
        for b in range(blocks):
            rows = pl.ds(b * BLOCK, BLOCK)
            part = dot(dk[h, rows, :], dv[h, rows, :], ((0,), (0,)))
            total = part if total is None else total + part
            cum[h, b] = total

    def make_scores(h):
        load(4, h).wait()
        rows = lax.broadcasted_iota(jnp.int32, (span, span), 0)
        columns = lax.broadcasted_iota(jnp.int32, (span, span), 1)
        keep = jnp.logical_and(rows >= columns, rows // BLOCK == columns // BLOCK)
        for s in range(tokens // span):
            part = pl.ds(s * span, span)
            block = dot(q[h, part, :], dk[h, part, :], ((1,), (1,)))
            block = jnp.where(keep, block, 0.0).astype(jnp.bfloat16)
            for i in range(span // BLOCK):
                near = slice(i * BLOCK, (i + 1) * BLOCK)
                scores[h, pl.ds(s * span + i * BLOCK, BLOCK), :] = block[near, near]

    def finish(h):
        carry = base[h] + p_in[h] + r_in[h]
        columns = pl.ds(pl.multiple_of(h * HEAD_DIM, HEAD_DIM), HEAD_DIM)
        gain = gain_ref[pl.ds(h, 1), :]
        for b in range(blocks):
            rows = pl.ds(b * BLOCK, BLOCK)
            state = carry if b == 0 else carry + cum[h, b - 1]
            left = jnp.concatenate([scores[h, rows, :], q[h, rows, :]], axis=1)
            right = jnp.concatenate([dv[h, rows, :], state.astype(jnp.bfloat16)], axis=0)
            attended = dot(left, right, ((1,), (0,)))
            inverse = lax.rsqrt(jnp.mean(attended * attended, axis=-1, keepdims=True) + 1e-06)
            out_ref[rows, columns] = (attended * inverse * gain).astype(jnp.bfloat16)

    def total(h):
        return cum[h, blocks - 1]

    ready = WIDE_LAG * jnp.maximum(w, wide - 1 - w)
    last = ready + NARROW_LAG * jnp.maximum(z, narrow - 1 - z)

    def slot(t, _):
        @pl.when(t < HEADS)
        def _():
            states(t)

        link(0, t - WIDE_LAG * w, lambda h: enc[h] + total(h))
        link(1, t - WIDE_LAG * (wide - 1 - w), lambda h: enc[h])

        @pl.when(inside(t - ready))
        def _():
            h = t - ready
            base[h] = enc[h] + f_in[h] + g_in[h]

        link(2, t - ready - NARROW_LAG * z, lambda h: base[h] + total(h))
        link(3, t - ready - NARROW_LAG * (narrow - 1 - z), lambda h: base[h])

        @pl.when(t < HEADS)
        def _():
            make_scores(t)

        @pl.when(inside(t - last))
        def _():
            finish(t - last)

        return 0

    slots = HEADS + WIDE_LAG * (wide - 1) + NARROW_LAG * (narrow - 1)
    lax.fori_loop(0, slots, slot, 0)

    for c in range(4):

        @pl.when(has[chains[c][3]])
        def _():
            for h in range(HEADS):
                remote(c, h).wait_send()


def local(wide, narrow, dec_queries, dec_keys, dec_values, enc_keys, enc_values, out_weight, head_gain):
    tokens = dec_queries.shape[0]
    blocks = tokens // BLOCK
    heads_in = pltpu.VMEM((HEADS, tokens, HEAD_DIM), jnp.bfloat16)
    state = pltpu.VMEM((HEADS, HEAD_DIM, HEAD_DIM), jnp.float32)
    normed = pl.pallas_call(
        functools.partial(kernel, wide, narrow),
        out_shape=jax.ShapeDtypeStruct((tokens, HEADS * HEAD_DIM), jnp.bfloat16),
        in_specs=[pl.BlockSpec(memory_space=pl.ANY)] * 5 + [pl.BlockSpec(memory_space=pltpu.VMEM)],
        out_specs=pl.BlockSpec(memory_space=pltpu.VMEM),
        scratch_shapes=[heads_in] * 5
        + [pltpu.VMEM((HEADS, tokens, BLOCK), jnp.bfloat16), state]
        + [pltpu.VMEM((HEADS, blocks, HEAD_DIM, HEAD_DIM), jnp.float32), state]
        + [state] * 8
        + [
            pltpu.SemaphoreType.DMA((5, HEADS)),
            pltpu.SemaphoreType.DMA((4, HEADS)),
            pltpu.SemaphoreType.DMA((4, HEADS)),
        ],
        compiler_params=pltpu.CompilerParams(
            collective_id=0, has_side_effects=True, vmem_limit_bytes=40 * 1024 * 1024
        ),
        cost_estimate=pl.CostEstimate(
            flops=5 * 2 * tokens * HEADS * HEAD_DIM * HEAD_DIM,
            bytes_accessed=6 * 2 * tokens * HEADS * HEAD_DIM,
            transcendentals=0,
        ),
    )(dec_queries, dec_keys, dec_values, enc_keys, enc_values, head_gain.reshape(HEADS, HEAD_DIM))
    return jnp.dot(normed, out_weight, preferred_element_type=jnp.float32).astype(jnp.bfloat16)


def solution(mesh):
    tokens = P(("books", "wide", "narrow"), None)
    return jax.shard_map(
        functools.partial(local, mesh.shape["wide"], mesh.shape["narrow"]),
        mesh=mesh,
        in_specs=(tokens,) * 5 + (P(), P()),
        out_specs=tokens,
        check_vma=False,
    )
```

time: 194 us -> 47.5 us (0.24)
  waiting for transfers between devices: 154 us -> 0 us
  Pallas kernels: 0 us -> 36.7 us
  between operations: 13.3 us -> 0.02 us
  matrix products: 14.3 us -> 3.68 us
  local copies, waits for them, and re-layouts: 9.38 us -> 6.81 us
  other arithmetic: 2.01 us -> 0 us
    psum x2 -> x0, waiting for transfers between devices: 88.9 us -> none  [the longest x1 53.4 us: local(): group_dec, group_enc = lax.psum((own_total, enc_part), 'narrow')]
    all_gather x2 -> x0, waiting for transfers between devices: 64.3 us -> none  [carried_in(): gathered = lax.all_gather(part, axis)]
    pallas_call x0 -> x1, Pallas kernels: none -> 36.7 us  [local(): pl.pallas_call(functools.partial(kernel, wide, narrow), out_shape=jax.Sha...]
    dot_general x4 -> x0, matrix products: 8.46 us -> none  [the longest x1 3.72 us: local(): jnp.einsum('nhcs,nshe->nche', scores_bf, values_dec, preferred_element_ty...]
    reshape x2 -> x0, local copies, waits for them, and re-layouts: 2.29 us -> none  [the longest x1 1.5 us: local(): enc_keys.reshape(tokens, HEADS, HEAD_DIM)]
    dot_general x1, matrix products: 5.85 us -> 3.68 us  [local(): jnp.dot(normed, out_weight, preferred_element_type=jnp.float32)]
    unnamed x13 -> x14, local copies, waits for them, and re-layouts: 6.3 us -> 6.81 us
  transfers between devices with their start and end apart: 4 -> 0, of which waited for: 4 -> 0; matrix products, arithmetic and copies ran while one was open for 4% -> 0% of each run, Pallas kernels for 0% -> 0%
where the time goes in v1:
time: 47.5 us; the launch traced here: 47.2 us
  Pallas kernels  36.7 us (77%)
  local copies, waits for them, and re-layouts  6.81 us (14%)
  matrix products  3.68 us (8%)
    pallas_call x1, Pallas kernels, local(): pl.pallas_call(functools.partial(kernel, wide, narrow), out_shape=jax.Sha...  36.7 us
    unnamed x14, local copies, waits for them, and re-layouts  6.81 us
    dot_general x1, matrix products, local(): jnp.dot(normed, out_weight, preferred_element_type=jnp.float32)  3.68 us

profile of v1, /device:TPU:0, one launch (start us, length us, event | category | flops | bytes accessed | tf_op | source)
XLA Modules:
  0.0 47.2 jit_solution(8501046779883678002)
XLA Ops:
  0.0 0.0 copy-start
  0.0 1.2 %copy-done = bf16[512,1024]{1,0:T(8,128)(2,1)S(1)} copy-done((bf16[512,1024]{1,0:T(8,128)(2,1)S(1)}, bf16[512,1024]{1,0:T(8,128)(2,1)}, u32[]{:S(2)}) %copy-start) | copy-done | bytes 1048600
  1.2 0.0 copy-start.1
  1.2 1.2 %copy-done.1 = bf16[512,1024]{1,0:T(8,128)(2,1)S(1)} copy-done((bf16[512,1024]{1,0:T(8,128)(2,1)S(1)}, bf16[512,1024]{1,0:T(8,128)(2,1)}, u32[]{:S(2)}) %copy-start.1) | copy-done | bytes 1048600
  2.5 0.0 copy-start.2
  2.5 1.2 %copy-done.2 = bf16[512,1024]{1,0:T(8,128)(2,1)S(1)} copy-done((bf16[512,1024]{1,0:T(8,128)(2,1)S(1)}, bf16[512,1024]{1,0:T(8,128)(2,1)}, u32[]{:S(2)}) %copy-start.2) | copy-done | bytes 1048600
  3.7 0.0 copy-start.3
  3.7 1.2 %copy-done.3 = bf16[512,1024]{1,0:T(8,128)(2,1)S(1)} copy-done((bf16[512,1024]{1,0:T(8,128)(2,1)S(1)}, bf16[512,1024]{1,0:T(8,128)(2,1)}, u32[]{:S(2)}) %copy-start.3) | copy-done | bytes 1048600
  4.9 0.0 copy-start.4
  4.9 1.2 %copy-done.4 = bf16[512,1024]{1,0:T(8,128)(2,1)S(1)} copy-done((bf16[512,1024]{1,0:T(8,128)(2,1)S(1)}, bf16[512,1024]{1,0:T(8,128)(2,1)}, u32[]{:S(2)}) %copy-start.4) | copy-done | bytes 1048600
  6.1 0.0 copy-start.5
  6.1 0.7 %copy-done.5 = f32[1024]{0:T(1024)S(1)} copy-done((f32[1024]{0:T(1024)S(1)}, f32[1024]{0:T(1024)}, u32[]{:S(2)}) %copy-start.5) | copy-done | bytes 4120
  6.8 0.0 copy-start.6
  6.8 36.7 %shard_map.73 = bf16[512,1024]{1,0:T(8,128)(2,1)S(1)} custom-call(bf16[512,1024]{1,0:T(8,128)(2,1)S(1)} %copy-done, bf16[512,1024]{1,0:T(8,128)(2,1)S(1)} %copy-done.1, bf16[512,1024]{1,0:T(8,128)(2,1)S(1)} %copy-done.2, bf16[512,1024]{1,0:T(8,128)(2,1)S(1)} %copy-done.3, bf16[512,1024]{1,0:T(8,128)(2,1)S(1)} %copy-done.4, f32[8,128]{1,0:T(8,128)S(1)} %bitcast.3), custom_call_target="tpu_custom_call" | custom-call | flops 671088640 | bytes 6291456 | tf_op jit(solution)/shard_map/pallas_call | solution.py:183
  43.5 0.0 copy-done.6
  43.5 3.7 %convolution_convert_fusion = bf16[512,2048]{1,0:T(8,128)(2,1)} fusion(bf16[512,1024]{1,0:T(8,128)(2,1)S(1)} %shard_map.73, bf16[1024,2048]{1,0:T(8,128)(2,1)S(1)} %copy-done.6), kind=kOutput, calls=%fused_computation | convolution fusion | flops 2148532224 | bytes 7340032 | tf_op jit(solution)/shard_map/dot_general | solution.py:206
Async XLA Ops:
  0.0 1.2 %copy-start = (bf16[512,1024]{1,0:T(8,128)(2,1)S(1)}, bf16[512,1024]{1,0:T(8,128)(2,1)}, u32[]{:S(2)}) copy-start(bf16[512,1024]{1,0:T(8,128)(2,1)} %q_hbm.1) | copy-start | bytes 3145732
  1.2 1.2 %copy-start.1 = (bf16[512,1024]{1,0:T(8,128)(2,1)S(1)}, bf16[512,1024]{1,0:T(8,128)(2,1)}, u32[]{:S(2)}) copy-start(bf16[512,1024]{1,0:T(8,128)(2,1)} %dk_hbm.1) | copy-start | bytes 3145732
  2.5 1.2 %copy-start.2 = (bf16[512,1024]{1,0:T(8,128)(2,1)S(1)}, bf16[512,1024]{1,0:T(8,128)(2,1)}, u32[]{:S(2)}) copy-start(bf16[512,1024]{1,0:T(8,128)(2,1)} %dv_hbm.1) | copy-start | bytes 3145732
  3.7 1.2 %copy-start.3 = (bf16[512,1024]{1,0:T(8,128)(2,1)S(1)}, bf16[512,1024]{1,0:T(8,128)(2,1)}, u32[]{:S(2)}) copy-start(bf16[512,1024]{1,0:T(8,128)(2,1)} %ek_hbm.1) | copy-start | bytes 3145732
  4.9 1.2 %copy-start.4 = (bf16[512,1024]{1,0:T(8,128)(2,1)S(1)}, bf16[512,1024]{1,0:T(8,128)(2,1)}, u32[]{:S(2)}) copy-start(bf16[512,1024]{1,0:T(8,128)(2,1)} %ev_hbm.1) | copy-start | bytes 3145732
  6.1 0.7 %copy-start.5 = (f32[1024]{0:T(1024)S(1)}, f32[1024]{0:T(1024)}, u32[]{:S(2)}) copy-start(f32[1024]{0:T(1024)} %param.13) | copy-start | bytes 12292
  6.8 36.7 %copy-start.6 = (bf16[1024,2048]{1,0:T(8,128)(2,1)S(1)}, bf16[1024,2048]{1,0:T(8,128)(2,1)}, u32[]{:S(2)}) copy-start(bf16[1024,2048]{1,0:T(8,128)(2,1)} %param.12) | copy-start | bytes 12582916

commit v2 on v1

v2 whole, which is shorter than its diff:
```python
import functools

import jax
import jax.numpy as jnp
from jax import lax
from jax.experimental import pallas as pl
from jax.experimental.pallas import tpu as pltpu
from jax.sharding import PartitionSpec as P

HEADS = 8
HEAD_DIM = 128
BLOCK = 128
PIECES = 2
ROWS = HEAD_DIM // PIECES
CHUNKS = HEADS * PIECES
GROUP = 2
GROUPS = HEADS // GROUP
WIDE_LAG = 4
NARROW_LAG = 5
PROJECT_TILE = 512
MESH = pl.DeviceIdType.MESH


def dot(a, b, contract):
    return lax.dot_general(a, b, (contract, ((), ())), preferred_element_type=jnp.float32)


def kernel(
    wide, narrow,
    q_hbm, dk_hbm, dv_hbm, ek_hbm, ev_hbm, weight_hbm, gain_hbm, out_ref,
    q, dk, dv, ek, ev, weight, gain, scores, normed, acc, enc, total, cum, base,
    f_out, g_out, p_out, r_out, f_in, g_in, p_in, r_in,
    load_sem, weight_sem, gain_sem, send_sem, recv_sem,
):
    w = lax.axis_index("wide")
    z = lax.axis_index("narrow")
    tokens = q.shape[1]
    blocks = tokens // BLOCK
    span = 2 * BLOCK if blocks % 2 == 0 else BLOCK
    group = GROUP * HEAD_DIM

    def load(i, h):
        src, dst = ((ek_hbm, ek), (ev_hbm, ev), (dk_hbm, dk), (dv_hbm, dv), (q_hbm, q))[i]
        columns = pl.ds(pl.multiple_of(h * HEAD_DIM, HEAD_DIM), HEAD_DIM)
        return pltpu.make_async_copy(src.at[:, columns], dst.at[h], load_sem.at[i, h])

    def load_weight(g):
        rows = pl.ds(pl.multiple_of(g * group, group), group)
        return pltpu.make_async_copy(weight_hbm.at[rows, :], weight.at[rows, :], weight_sem.at[g])

    load_gain = pltpu.make_async_copy(gain_hbm, gain, gain_sem)

    def fetch(h):
        for i in range(5):
            load(i, h).start()

    def states(h):
        for i in range(4):
            load(i, h).wait()
        pieces = pl.ds(h * PIECES, PIECES)
        enc[pieces] = dot(ek[h], ev[h], ((0,), (0,))).reshape(PIECES, ROWS, HEAD_DIM)
        so_far = None
        for b in range(blocks):
            rows = pl.ds(b * BLOCK, BLOCK)
            part = dot(dk[h, rows, :], dv[h, rows, :], ((0,), (0,)))
            so_far = part if so_far is None else so_far + part
            if b < blocks - 1:
                cum[h, b] = so_far
        total[pieces] = so_far.reshape(PIECES, ROWS, HEAD_DIM)

    barrier = pltpu.get_barrier_semaphore()
    has = (w > 0, w < wide - 1, z > 0, z < narrow - 1)
    peers = ({"wide": w - 1}, {"wide": w + 1}, {"narrow": z - 1}, {"narrow": z + 1})
    fetch(0)
    for there, peer in zip(has, peers):

        @pl.when(there)
        def _():
            pl.semaphore_signal(barrier, inc=1, device_id=peer, device_id_type=MESH)

    fetch(1)
    fetch(2)
    load_gain.start()

    for there, ref in zip(has, (f_in, g_in, p_in, r_in)):

        @pl.when(jnp.logical_not(there))
        def _():
            ref[...] = jnp.zeros_like(ref)

    states(0)
    load_gain.wait()
    pl.semaphore_wait(barrier, sum(there.astype(jnp.int32) for there in has))

    chains = (
        (f_out, f_in, 0, 1),
        (g_out, g_in, 1, 0),
        (p_out, p_in, 2, 3),
        (r_out, r_in, 3, 2),
    )

    def remote(c, n):
        out, into, _, to = chains[c]
        return pltpu.make_async_remote_copy(
            src_ref=out.at[n],
            dst_ref=into.at[n],
            send_sem=send_sem.at[c, n],
            recv_sem=recv_sem.at[c, n],
            device_id=peers[to],
            device_id_type=MESH,
        )

    def inside(n):
        return jnp.logical_and(n >= 0, n < CHUNKS)

    def link(c, n, value):
        out, into, source, to = chains[c]

        @pl.when(inside(n))
        def _():
            @pl.when(has[source])
            def _():
                remote(c, n).wait_recv()

            @pl.when(has[to])
            def _():
                out[n] = into[n] + value(n)
                remote(c, n).start()

    def make_scores(h):
        load(4, h).wait()
        rows = lax.broadcasted_iota(jnp.int32, (span, span), 0)
        columns = lax.broadcasted_iota(jnp.int32, (span, span), 1)
        keep = jnp.logical_and(rows >= columns, rows // BLOCK == columns // BLOCK)
        for s in range(tokens // span):
            part = pl.ds(s * span, span)
            block = dot(q[h, part, :], dk[h, part, :], ((1,), (1,)))
            block = jnp.where(keep, block, 0.0).astype(jnp.bfloat16)
            for i in range(span // BLOCK):
                near = slice(i * BLOCK, (i + 1) * BLOCK)
                scores[h, pl.ds(s * span + i * BLOCK, BLOCK), :] = block[near, near]

    def finish(h):
        pieces = pl.ds(h * PIECES, PIECES)
        carry = (base[pieces] + p_in[pieces] + r_in[pieces]).reshape(HEAD_DIM, HEAD_DIM)
        columns = pl.ds(pl.multiple_of(h * HEAD_DIM, HEAD_DIM), HEAD_DIM)
        for b in range(blocks):
            rows = pl.ds(b * BLOCK, BLOCK)
            state = carry if b == 0 else carry + cum[h, b - 1]
            left = jnp.concatenate([scores[h, rows, :], q[h, rows, :]], axis=1)
            right = jnp.concatenate([dv[h, rows, :], state.astype(jnp.bfloat16)], axis=0)
            attended = dot(left, right, ((1,), (0,)))
            inverse = lax.rsqrt(jnp.mean(attended * attended, axis=-1, keepdims=True) + 1e-06)
            normed[rows, columns] = (attended * inverse * gain[pl.ds(h, 1), :]).astype(jnp.bfloat16)

    def project(g):
        depth = pl.ds(pl.multiple_of(g * group, group), group)
        load_weight(g).wait()
        tile = min(PROJECT_TILE, out_ref.shape[1])

        def over(store):
            for j in range(out_ref.shape[1] // tile):
                columns = slice(j * tile, (j + 1) * tile)
                store(columns, dot(normed[:, depth], weight[depth, columns], ((1,), (0,))))

        @pl.when(g == 0)
        def _():
            def store(columns, value):
                acc[:, columns] = value

            over(store)

        @pl.when(jnp.logical_and(g > 0, g < GROUPS - 1))
        def _():
            def store(columns, value):
                acc[:, columns] += value

            over(store)

        @pl.when(g == GROUPS - 1)
        def _():
            def store(columns, value):
                out_ref[:, columns] = (acc[:, columns] + value).astype(jnp.bfloat16)

            over(store)

    ready = WIDE_LAG * jnp.maximum(w, wide - 1 - w)
    last = ready + NARROW_LAG * jnp.maximum(z, narrow - 1 - z)

    def slot(t, _):
        h = t // PIECES
        live = jnp.logical_and(h < HEADS, t % PIECES == 0)

        @pl.when(jnp.logical_and(live, h > 0))
        def _():
            states(h)

        link(0, t - WIDE_LAG * w, lambda n: enc[n] + total[n])
        link(1, t - WIDE_LAG * (wide - 1 - w), lambda n: enc[n])

        @pl.when(inside(t - ready))
        def _():
            n = t - ready
            base[n] = enc[n] + f_in[n] + g_in[n]

        link(2, t - ready - NARROW_LAG * z, lambda n: base[n] + total[n])
        link(3, t - ready - NARROW_LAG * (narrow - 1 - z), lambda n: base[n])

        @pl.when(live)
        def _():
            @pl.when(h + 3 < HEADS)
            def _():
                fetch(h + 3)

        after = t - (PIECES - 1)

        @pl.when(jnp.logical_and(after >= 0, jnp.logical_and(after // PIECES < HEADS, after % PIECES == 0)))
        def _():
            make_scores(after // PIECES)

        early = t // (GROUP * PIECES)

        @pl.when(jnp.logical_and(early < GROUPS, t % (GROUP * PIECES) == 0))
        def _():
            load_weight(early).start()

        n = t - last
        done = n - (PIECES - 1)

        @pl.when(jnp.logical_and(done >= 0, jnp.logical_and(done // PIECES < HEADS, done % PIECES == 0)))
        def _():
            finish(done // PIECES)

        whole = n - (GROUP * PIECES - 1)

        @pl.when(
            jnp.logical_and(
                whole >= 0, jnp.logical_and(whole < CHUNKS, whole % (GROUP * PIECES) == 0)
            )
        )
        def _():
            project(whole // (GROUP * PIECES))

        return 0

    slots = CHUNKS + WIDE_LAG * (wide - 1) + NARROW_LAG * (narrow - 1)
    lax.fori_loop(0, slots, slot, 0)

    for c in range(4):

        @pl.when(has[chains[c][3]])
        def _():
            for n in range(CHUNKS):
                remote(c, n).wait_send()


def local(wide, narrow, dec_queries, dec_keys, dec_values, enc_keys, enc_values, out_weight, head_gain):
    tokens = dec_queries.shape[0]
    blocks = tokens // BLOCK
    depth, model = out_weight.shape
    heads_in = pltpu.VMEM((HEADS, tokens, HEAD_DIM), jnp.bfloat16)
    state = pltpu.VMEM((CHUNKS, ROWS, HEAD_DIM), jnp.float32)
    held = [
        pltpu.with_memory_space_constraint(x, pltpu.HBM)
        for x in (dec_queries, dec_keys, dec_values, enc_keys, enc_values, out_weight)
    ]
    gain = pltpu.with_memory_space_constraint(head_gain.reshape(HEADS, HEAD_DIM), pltpu.HBM)
    return pl.pallas_call(
        functools.partial(kernel, wide, narrow),
        out_shape=jax.ShapeDtypeStruct((tokens, model), jnp.bfloat16),
        in_specs=[pl.BlockSpec(memory_space=pltpu.HBM)] * 7,
        out_specs=pl.BlockSpec(memory_space=pltpu.VMEM),
        scratch_shapes=[heads_in] * 5
        + [
            pltpu.VMEM((depth, model), jnp.bfloat16),
            pltpu.VMEM((HEADS, HEAD_DIM), jnp.float32),
            pltpu.VMEM((HEADS, tokens, BLOCK), jnp.bfloat16),
            pltpu.VMEM((tokens, depth), jnp.bfloat16),
            pltpu.VMEM((tokens, model), jnp.float32),
            state,
            state,
            pltpu.VMEM((HEADS, max(blocks - 1, 1), HEAD_DIM, HEAD_DIM), jnp.float32),
            state,
        ]
        + [state] * 8
        + [
            pltpu.SemaphoreType.DMA((5, HEADS)),
            pltpu.SemaphoreType.DMA((GROUPS,)),
            pltpu.SemaphoreType.DMA,
            pltpu.SemaphoreType.DMA((4, CHUNKS)),
            pltpu.SemaphoreType.DMA((4, CHUNKS)),
        ],
        compiler_params=pltpu.CompilerParams(
            collective_id=0, has_side_effects=True, vmem_limit_bytes=48 * 1024 * 1024
        ),
    )(*held, gain)


def solution(mesh):
    tokens = P(("books", "wide", "narrow"), None)
    return jax.shard_map(
        functools.partial(local, mesh.shape["wide"], mesh.shape["narrow"]),
        mesh=mesh,
        in_specs=(tokens,) * 5 + (P(), P()),
        out_specs=tokens,
        check_vma=False,
    )
```

time: 47.5 us -> 33.7 us (0.71)
  local copies, waits for them, and re-layouts: 6.81 us -> 1.32 us
  Pallas kernels: 36.7 us -> 32.2 us
  matrix products: 3.68 us -> 0 us
    unnamed x14 -> x1, local copies, waits for them, and re-layouts: 6.81 us -> 1.32 us
    pallas_call x1, Pallas kernels: 36.7 us -> 32.2 us  [local(): pl.pallas_call(functools.partial(kernel, wide, narrow), out_shape=jax.Sha...]
    dot_general x1 -> x0, matrix products: 3.68 us -> none  [local(): jnp.dot(normed, out_weight, preferred_element_type=jnp.float32)]
where the time goes in v2:
time: 33.7 us; the launch traced here: 33.5 us
  Pallas kernels  32.2 us (96%)
  local copies, waits for them, and re-layouts  1.32 us (4%)
    pallas_call x1, Pallas kernels, local(): pl.pallas_call(functools.partial(kernel, wide, narrow), out_shape=jax.Sha...  32.2 us
    unnamed x1, local copies, waits for them, and re-layouts  1.32 us

profile of v2, /device:TPU:0, one launch (start us, length us, event | category | flops | bytes accessed | tf_op | source)
XLA Modules:
  0.0 33.5 jit_solution(15117271431442691332)
XLA Ops:
  0.0 32.2 %shard_map.73 = bf16[512,2048]{1,0:T(8,128)(2,1)S(1)} custom-call(bf16[512,1024]{1,0:T(8,128)(2,1)} %q_hbm.1, bf16[512,1024]{1,0:T(8,128)(2,1)} %dk_hbm.1, bf16[512,1024]{1,0:T(8,128)(2,1)} %dv_hbm.1, bf16[512,1024]{1,0:T(8,128)(2,1)} %ek_hbm.1, bf16[512,1024]{1,0:T(8,128)(2,1)} %ev_hbm.1, bf16[1024,2048]{1,0:T(8,128)(2,1)} %weight_hbm.1, f32[8,128]{1,0:T(8,128)} %bitcast.1), custom_call_target="tpu_custom_call" | custom-call | tf_op jit(solution)/shard_map/pallas_call | solution.py:268
  32.2 1.3 %copy.9 = bf16[512,2048]{1,0:T(8,128)(2,1)} copy(bf16[512,2048]{1,0:T(8,128)(2,1)S(1)} %shard_map.73) | data formatting | bytes 4194304

commit v3 on v2

--- a/solution.py
+++ b/solution.py
@@ -10,14 +10,15 @@
 HEADS = 8
 HEAD_DIM = 128
 BLOCK = 128
-PIECES = 2
+PIECES = 1
 ROWS = HEAD_DIM // PIECES
 CHUNKS = HEADS * PIECES
 GROUP = 2
 GROUPS = HEADS // GROUP
-WIDE_LAG = 4
-NARROW_LAG = 5
+WIDE_LAG = 2
+NARROW_LAG = 3
 PROJECT_TILE = 512
+SCORES_AHEAD = 3
 MESH = pl.DeviceIdType.MESH
 
 
@@ -212,7 +213,7 @@
             def _():
                 fetch(h + 3)
 
-        after = t - (PIECES - 1)
+        after = t - jnp.maximum(last - SCORES_AHEAD, 0) - (PIECES - 1)
 
         @pl.when(jnp.logical_and(after >= 0, jnp.logical_and(after // PIECES < HEADS, after % PIECES == 0)))
         def _():

time: 33.7 us -> 33.3 us (0.988)
  Pallas kernels: 32.2 us -> 31.8 us
    pallas_call x1, Pallas kernels: 32.2 us -> 31.8 us  [local(): pl.pallas_call(functools.partial(kernel, wide, narrow), out_shape=jax.Sha...]
where the time goes in v3:
time: 33.3 us; the launch traced here: 33.2 us
  Pallas kernels  31.8 us (95%)
  local copies, waits for them, and re-layouts  1.32 us (4%)
    pallas_call x1, Pallas kernels, local(): pl.pallas_call(functools.partial(kernel, wide, narrow), out_shape=jax.Sha...  31.8 us
    unnamed x1, local copies, waits for them, and re-layouts  1.32 us

profile of v3, /device:TPU:0, one launch (start us, length us, event | category | flops | bytes accessed | tf_op | source)
XLA Modules:
  0.0 33.2 jit_solution(8678529821943696167)
XLA Ops:
  0.0 31.8 %shard_map.73 = bf16[512,2048]{1,0:T(8,128)(2,1)S(1)} custom-call(bf16[512,1024]{1,0:T(8,128)(2,1)} %q_hbm.1, bf16[512,1024]{1,0:T(8,128)(2,1)} %dk_hbm.1, bf16[512,1024]{1,0:T(8,128)(2,1)} %dv_hbm.1, bf16[512,1024]{1,0:T(8,128)(2,1)} %ek_hbm.1, bf16[512,1024]{1,0:T(8,128)(2,1)} %ev_hbm.1, bf16[1024,2048]{1,0:T(8,128)(2,1)} %weight_hbm.1, f32[8,128]{1,0:T(8,128)} %bitcast.1), custom_call_target="tpu_custom_call" | custom-call | tf_op jit(solution)/shard_map/pallas_call | solution.py:269
  31.8 1.3 %copy.9 = bf16[512,2048]{1,0:T(8,128)(2,1)} copy(bf16[512,2048]{1,0:T(8,128)(2,1)S(1)} %shard_map.73) | data formatting | bytes 4194304

commit v4 on v3

--- a/solution.py
+++ b/solution.py
@@ -15,7 +15,8 @@
 CHUNKS = HEADS * PIECES
 GROUP = 2
 GROUPS = HEADS // GROUP
-WIDE_LAG = 2
+NEAR_LAG = 1
+FAR_LAG = 3
 NARROW_LAG = 3
 PROJECT_TILE = 512
 SCORES_AHEAD = 3
@@ -185,7 +186,10 @@
 
             over(store)
 
-    ready = WIDE_LAG * jnp.maximum(w, wide - 1 - w)
+    def wide_lag(hops):
+        return NEAR_LAG * ((hops + 1) // 2) + FAR_LAG * (hops // 2)
+
+    ready = wide_lag(jnp.maximum(w, wide - 1 - w))
     last = ready + NARROW_LAG * jnp.maximum(z, narrow - 1 - z)
 
     def slot(t, _):
@@ -196,8 +200,8 @@
         def _():
             states(h)
 
-        link(0, t - WIDE_LAG * w, lambda n: enc[n] + total[n])
-        link(1, t - WIDE_LAG * (wide - 1 - w), lambda n: enc[n])
+        link(0, t - wide_lag(w), lambda n: enc[n] + total[n])
+        link(1, t - wide_lag(wide - 1 - w), lambda n: enc[n])
 
         @pl.when(inside(t - ready))
         def _():
@@ -244,7 +248,7 @@
 
         return 0
 
-    slots = CHUNKS + WIDE_LAG * (wide - 1) + NARROW_LAG * (narrow - 1)
+    slots = CHUNKS + NEAR_LAG * (wide // 2) + FAR_LAG * ((wide - 1) // 2) + NARROW_LAG * (narrow - 1)
     lax.fori_loop(0, slots, slot, 0)
 
     for c in range(4):

time: 33.3 us -> 32.7 us (0.982)
  Pallas kernels: 31.8 us -> 31.2 us
    pallas_call x1, Pallas kernels: 31.8 us -> 31.2 us  [local(): pl.pallas_call(functools.partial(kernel, wide, narrow), out_shape=jax.Sha...]
where the time goes in v4:
time: 32.7 us; the launch traced here: 32.5 us
  Pallas kernels  31.2 us (95%)
  local copies, waits for them, and re-layouts  1.32 us (4%)
    pallas_call x1, Pallas kernels, local(): pl.pallas_call(functools.partial(kernel, wide, narrow), out_shape=jax.Sha...  31.2 us
    unnamed x1, local copies, waits for them, and re-layouts  1.32 us

profile of v4, /device:TPU:0, one launch (start us, length us, event | category | flops | bytes accessed | tf_op | source)
XLA Modules:
  0.0 32.5 jit_solution(16719886970111276872)
XLA Ops:
  0.0 31.2 %shard_map.73 = bf16[512,2048]{1,0:T(8,128)(2,1)S(1)} custom-call(bf16[512,1024]{1,0:T(8,128)(2,1)} %q_hbm.1, bf16[512,1024]{1,0:T(8,128)(2,1)} %dk_hbm.1, bf16[512,1024]{1,0:T(8,128)(2,1)} %dv_hbm.1, bf16[512,1024]{1,0:T(8,128)(2,1)} %ek_hbm.1, bf16[512,1024]{1,0:T(8,128)(2,1)} %ev_hbm.1, bf16[1024,2048]{1,0:T(8,128)(2,1)} %weight_hbm.1, f32[8,128]{1,0:T(8,128)} %bitcast.1), custom_call_target="tpu_custom_call" | custom-call | tf_op jit(solution)/shard_map/pallas_call | solution.py:273
  31.2 1.3 %copy.9 = bf16[512,2048]{1,0:T(8,128)(2,1)} copy(bf16[512,2048]{1,0:T(8,128)(2,1)S(1)} %shard_map.73) | data formatting | bytes 4194304

commit v5 on v4

--- a/solution.py
+++ b/solution.py
@@ -16,7 +16,7 @@
 GROUP = 2
 GROUPS = HEADS // GROUP
 NEAR_LAG = 1
-FAR_LAG = 3
+FAR_LAG = 4
 NARROW_LAG = 3
 PROJECT_TILE = 512
 SCORES_AHEAD = 3

time: 32.7 us -> 32.7 us (level)
  no operation moved by 1% of the time
where the time goes in v5:
time: 32.7 us; the launch traced here: 32.6 us
  Pallas kernels  31.2 us (95%)
  local copies, waits for them, and re-layouts  1.32 us (4%)
    pallas_call x1, Pallas kernels, local(): pl.pallas_call(functools.partial(kernel, wide, narrow), out_shape=jax.Sha...  31.2 us
    unnamed x1, local copies, waits for them, and re-layouts  1.32 us

profile of v5, /device:TPU:0, one launch (start us, length us, event | category | flops | bytes accessed | tf_op | source)
XLA Modules:
  0.0 32.6 jit_solution(16841232644556284909)
XLA Ops:
  0.0 31.2 %shard_map.73 = bf16[512,2048]{1,0:T(8,128)(2,1)S(1)} custom-call(bf16[512,1024]{1,0:T(8,128)(2,1)} %q_hbm.1, bf16[512,1024]{1,0:T(8,128)(2,1)} %dk_hbm.1, bf16[512,1024]{1,0:T(8,128)(2,1)} %dv_hbm.1, bf16[512,1024]{1,0:T(8,128)(2,1)} %ek_hbm.1, bf16[512,1024]{1,0:T(8,128)(2,1)} %ev_hbm.1, bf16[1024,2048]{1,0:T(8,128)(2,1)} %weight_hbm.1, f32[8,128]{1,0:T(8,128)} %bitcast.1), custom_call_target="tpu_custom_call" | custom-call | tf_op jit(solution)/shard_map/pallas_call | solution.py:273
  31.2 1.3 %copy.9 = bf16[512,2048]{1,0:T(8,128)(2,1)} copy(bf16[512,2048]{1,0:T(8,128)(2,1)S(1)} %shard_map.73) | data formatting | bytes 4194304
